TPU v7x, 256 devices: a whole 4x4x8 slice. The times are simulated.
256 devices in a mesh: row: 16 (over z_lo, x), col: 16 (over y, z_hi, core).
Axes of the slice: x: 4, y: 4, z: 8 (z_hi: 2, z_lo: 4; z = z_hi * 4 + z_lo), core: 2. Of those that a mesh axis runs over, the one named last changes fastest.
Arguments:
- inverse_block: bfloat16 [10240, 10240], P('row', 'col'), may hold values from -6 to 6
- factor_cols: bfloat16 [10240, 4096], P('row', 'col'), may hold values from -0.078125 to 0.078125
- diag_inverse: float32 [16, 256, 256], P('col', 'row'), may hold values from -6 to 6
- fill_mask: int32 [40, 16], replicated, may hold values from 0 to 1
Outputs:
- inverse_cols: bfloat16 [10240, 4096], P('row', 'col')
- inverse_diag: float32 [16, 256, 256], P('col', 'row')
All inputs are finite; a program needn't handle non-finite values.
Results may differ from a plain program's by a relative error of at most 0.0027.
Values may be sent and summed in bfloat16 or wider, within the bound.
No kernel may reach another device: no remote copies, remote signals or barrier semaphores. Data moves between devices by JAX's collectives and lax.ppermute only.
A program may use at most 64 MiB of HBM per device.

v0:
```python
import jax
import jax.numpy as jnp
from jax import lax
from jax.sharding import PartitionSpec as P


def body(inverse_block, factor_cols, diag_inverse, fill_mask):
    rows_device, cols_device = factor_cols.shape
    nodes_device, diag_rows, block_width = diag_inverse.shape
    block_count, node_count = fill_mask.shape
    row_index = lax.axis_index("row")
    col_index = lax.axis_index("col")
    expanded = jnp.broadcast_to(
        fill_mask[:, None, :], (block_count, block_width, node_count)
    ).reshape(block_count * block_width, node_count)
    local_mask = lax.dynamic_slice(
        expanded, (row_index * rows_device, col_index * nodes_device), (rows_device, nodes_device)
    )
    column_mask = jnp.broadcast_to(
        local_mask[:, :, None], (rows_device, nodes_device, block_width)
    ).reshape(rows_device, cols_device)
    selected = factor_cols * column_mask.astype(jnp.bfloat16)
    gathered_panel = lax.all_gather(selected, "row", axis=0, tiled=True)
    spread = lax.all_to_all(gathered_panel, "col", split_axis=0, concat_axis=1, tiled=True)
    partial_value = jnp.dot(inverse_block, spread, preferred_element_type=jnp.float32)
    summed = lax.psum_scatter(partial_value, "col", scatter_dimension=1, tiled=True)
    inverse_cols = (-summed * column_mask.astype(jnp.float32)).astype(jnp.bfloat16)
    left_side = selected.reshape(rows_device, nodes_device, block_width)
    right_side = inverse_cols.reshape(rows_device, nodes_device, block_width)
    correction = jnp.einsum(
        "isa,isb->sab", left_side, right_side, preferred_element_type=jnp.float32
    )
    shared = lax.psum_scatter(correction, "row", scatter_dimension=1, tiled=True)
    inverse_diag = diag_inverse - shared
    return (inverse_cols, inverse_diag)


def solution(mesh):
    placed = (P("row", "col"), P("row", "col"), P("col", "row", None), P())
    return jax.shard_map(
        body,
        mesh=mesh,
        in_specs=placed,
        out_specs=(P("row", "col"), P("col", "row", None)),
        check_vma=False,
    )
```

profile of v0, /device:TPU:8, one launch (start us, length us, event | category | flops | bytes accessed | tf_op | source)
XLA Modules:
  0.0 491.6 jit_solution(3186827072917401955)
XLA Ops:
  7.2 0.0 copy-start
  7.2 0.0 all-gather.2.cloned.1.call-start
  7.2 0.9 broadcast_in_dim.2
  8.1 0.2 copy.11
  8.4 0.1 convert_reduce_fusion.1
  8.5 1.9 broadcast_multiply_fusion
  10.3 0.0 all-gather.2.cloned.1.call-update
  10.3 0.0 reduce-scatter.3.cloned.1.call-start
  10.4 92.8 %all-gather.2.cloned.1.call-done = bf16[10240,256]{1,0:T(8,128)(2,1)} async-done(((bf16[640,256]{1,0:T(8,128)(2,1)}), bf16[10240,256]{1,0:T(8,128)(2,1)}) %all-gather.2.cloned.1.call-update) | async-done | bytes 5242896 | tf_op jit(solution)/shard_map/all_gather | solution.py:23
  103.2 117.7 %all_to_all.19 = bf16[16,640,256]{2,1,0:T(8,128)(2,1)} all-to-all(bf16[16,640,256]{2,1,0:T(8,128)(2,1)} %bitcast.16), channel_id=1, replica_groups=mesh['row'=16,'col'=16] {'col'}, dimensions={0} | all-to-all | bytes 10485760 | tf_op jit(solution)/shard_map/all_to_all | solution.py:24
  220.9 7.9 %copy.9 = bf16[640,16,256]{0,2,1:T(8,128)(2,1)} copy(bf16[640,16,256]{2,0,1:T(8,128)(2,1)} %bitcast.15) | data formatting | bytes 10485760 | tf_op jit(solution)/shard_map/all_to_all | solution.py:24
  228.8 0.0 copy-done
  228.8 9.7 %convolution_bitcast_fusion = f32[640,4096]{0,1:T(8,128)} fusion(bf16[640,4096]{0,1:T(8,128)(2,1)} %bitcast.17, bf16[640,640]{1,0:T(8,128)(2,1)S(1)} %copy-done), kind=kOutput, calls=%fused_computation | convolution fusion | flops 3355443200 | bytes 16547840 | tf_op jit(solution)/shard_map/dot_general | solution.py:25
  238.5 0.0 copy-start.1
  238.5 0.0 copy-start.2
  238.5 0.0 reduce-scatter.3.cloned.1.call-update
  238.5 0.0 reduce-scatter.5.cloned.1.call-start
  238.6 0.1 convert_reduce_fusion
  238.7 161.4 %reduce-scatter.3.cloned.1.call-done = f32[640,256]{0,1:T(8,128)} async-done(((f32[640,4096]{0,1:T(8,128)}), f32[640,256]{0,1:T(8,128)}) %reduce-scatter.3.cloned.1.call-update) | async-done | bytes 655376 | tf_op jit(solution)/shard_map/reduce_scatter | solution.py:26
  400.0 1.1 multiply_convert_fusion
  401.2 0.0 copy-done.1
  401.2 1.0 convolution_bitcast_fusion.1
  402.2 0.0 reduce-scatter.5.cloned.1.call-update
  402.2 0.9 copy.10
  403.1 80.6 %reduce-scatter.5.cloned.1.call-done = f32[1,16,256]{2,1,0:T(8,128)} async-done(((f32[1,256,256]{2,1,0:T(8,128)}), f32[1,16,256]{2,1,0:T(8,128)}) %reduce-scatter.5.cloned.1.call-update) | async-done | bytes 16400 | tf_op jit(solution)/shard_map/reduce_scatter | solution.py:33
  483.7 0.0 copy-done.2
  483.7 1.3 sub.3
Async XLA Ops:
  7.2 221.6 %copy-start = (bf16[640,640]{1,0:T(8,128)(2,1)S(1)}, bf16[640,640]{1,0:T(8,128)(2,1)}, u32[]{:S(2)}) copy-start(bf16[640,640]{1,0:T(8,128)(2,1)} %param.4) | copy-start | bytes 2457604
  7.2 96.0 %all-gather.2.cloned.1.call-start = ((), (), s32[]{:S(2)}) async-start(), calls=%async_computation.3 | async-start | bytes 5570560 | tf_op jit(solution)/shard_map/all_gather | solution.py:23
  10.3 389.7 %reduce-scatter.3.cloned.1.call-start = ((), (), s32[]{:S(2)}) async-start(), calls=%async_computation.4 | async-start | bytes 11141120 | tf_op jit(solution)/shard_map/reduce_scatter | solution.py:26
  238.5 162.7 %copy-start.1 = (bf16[640,256]{1,0:T(8,128)(2,1)S(1)}, bf16[640,256]{1,0:T(8,128)(2,1)}, u32[]{:S(2)}) copy-start(bf16[640,256]{1,0:T(8,128)(2,1)} %broadcast_multiply_fusion) | copy-start | bytes 983044
  238.5 245.2 %copy-start.2 = (f32[1,16,256]{2,1,0:T(8,128)S(1)}, f32[1,16,256]{2,1,0:T(8,128)}, u32[]{:S(2)}) copy-start(f32[1,16,256]{2,1,0:T(8,128)} %param.6) | copy-start | bytes 49156
  238.5 245.2 %reduce-scatter.5.cloned.1.call-start = ((), (), s32[]{:S(2)}) async-start(), calls=%async_computation.5 | async-start | bytes 278528 | tf_op jit(solution)/shard_map/reduce_scatter | solution.py:33
Sparse Core Ops, SparseCore 0:
  10.4 92.7 all-gather.1
  238.7 161.3 reduce-scatter.2
  402.5 81.1 reduce-scatter.4
where the time goes:
time: 492 us
  waiting for transfers between devices  335 us (68%)
  blocking collectives  118 us (24%)
  between operations  13.8 us (3%)
  matrix products  10.7 us (2%)
  local copies, waits for them, and re-layouts  9.88 us (2%)
    reduce_scatter x1, waiting for transfers between devices, body(): lax.psum_scatter(partial_value, 'col', scatter_dimension=1, tiled=True)  161 us
    all_to_all x1, blocking collectives, body(): lax.all_to_all(gathered_panel, 'col', split_axis=0, concat_axis=1, tiled=...  118 us
    all_gather x1, waiting for transfers between devices, body(): gathered_panel = lax.all_gather(selected, 'row', axis=0, tiled=True)  92.8 us
    reduce_scatter x1, waiting for transfers between devices, body(): lax.psum_scatter(correction, 'row', scatter_dimension=1, tiled=True)  80.6 us
  transfers between devices with their start and end apart: 3, of which 3 were waited for; matrix products, arithmetic and copies ran while one was open for 0% of the time, Pallas kernels for 0%

commit v1 on v0

--- a/solution.py
+++ b/solution.py
@@ -20,7 +20,10 @@
         local_mask[:, :, None], (rows_device, nodes_device, block_width)
     ).reshape(rows_device, cols_device)
     selected = factor_cols * column_mask.astype(jnp.bfloat16)
-    gathered_panel = lax.all_gather(selected, "row", axis=0, tiled=True)
+    count = lax.axis_size("row")
+    tiles = jnp.stack([selected for _ in range(count)])
+    tiles = lax.all_to_all(tiles, "row", split_axis=0, concat_axis=0)
+    gathered_panel = jnp.concatenate(tiles, axis=0)
     spread = lax.all_to_all(gathered_panel, "col", split_axis=0, concat_axis=1, tiled=True)
     partial_value = jnp.dot(inverse_block, spread, preferred_element_type=jnp.float32)
     summed = lax.psum_scatter(partial_value, "col", scatter_dimension=1, tiled=True)

time: 492 us -> 518 us (1.053)
  blocking collectives: 118 us -> 201 us
  waiting for transfers between devices: 335 us -> 288 us
  local copies, waits for them, and re-layouts: 9.88 us -> 2.83 us
    all_to_all x0 -> x1, blocking collectives: none -> 125 us  [body(): tiles = lax.all_to_all(tiles, 'row', split_axis=0, concat_axis=0)]
    all_gather x1 -> x0, waiting for transfers between devices: 92.8 us -> none  [body(): gathered_panel = lax.all_gather(selected, 'row', axis=0, tiled=True)]
    reduce_scatter x1, waiting for transfers between devices: 161 us -> 207 us  [body(): lax.psum_scatter(partial_value, 'col', scatter_dimension=1, tiled=True)]
    all_to_all x1, blocking collectives: 118 us -> 76.2 us  [body(): lax.all_to_all(gathered_panel, 'col', split_axis=0, concat_axis=1, tiled=...]
    all_to_all x1 -> x0, local copies, waits for them, and re-layouts: 7.86 us -> none  [body(): lax.all_to_all(gathered_panel, 'col', split_axis=0, concat_axis=1, tiled=...]
  transfers between devices with their start and end apart: 3 -> 2, of which waited for: 3 -> 2; matrix products, arithmetic and copies ran while one was open for 0% -> 0% of each run, Pallas kernels for 0% -> 0%
where the time goes in v1:
time: 518 us
  waiting for transfers between devices  288 us (56%)
  blocking collectives  201 us (39%)
  between operations  14.1 us (3%)
  matrix products  8.34 us (2%)
    reduce_scatter x1, waiting for transfers between devices, body(): lax.psum_scatter(partial_value, 'col', scatter_dimension=1, tiled=True)  207 us
    all_to_all x1, blocking collectives, body(): tiles = lax.all_to_all(tiles, 'row', split_axis=0, concat_axis=0)  125 us
    reduce_scatter x1, waiting for transfers between devices, body(): lax.psum_scatter(correction, 'row', scatter_dimension=1, tiled=True)  80.6 us
    all_to_all x1, blocking collectives, body(): lax.all_to_all(gathered_panel, 'col', split_axis=0, concat_axis=1, tiled=...  76.2 us
  transfers between devices with their start and end apart: 2, of which 2 were waited for; matrix products, arithmetic and copies ran while one was open for 0% of the time, Pallas kernels for 0%

profile of v1, /device:TPU:8, one launch (start us, length us, event | category | flops | bytes accessed | tf_op | source)
XLA Modules:
  0.0 517.8 jit_solution(9733966588426952832)
XLA Ops:
  7.2 0.0 copy-start
  7.2 0.0 reduce-scatter.3.cloned.1.call-start
  7.2 0.9 broadcast_in_dim.2
  8.1 0.2 copy.10
  8.3 0.1 convert_reduce_fusion.1
  8.4 1.1 broadcast_multiply_fusion
  9.6 0.2 copy.8
  9.8 0.6 stack.2
  10.4 124.8 %all_to_all.21 = bf16[16,640,256]{1,2,0:T(8,128)(2,1)S(1)} all-to-all(bf16[16,640,256]{1,2,0:T(8,128)(2,1)S(1)} %stack.2), channel_id=1, replica_groups=mesh['row'=16,'col'=16] {'row'}, dimensions={0} | all-to-all | bytes 10485760 | tf_op jit(solution)/shard_map/all_to_all | solution.py:25
  135.2 76.2 %all_to_all.22 = bf16[16,640,256]{1,2,0:T(8,128)(2,1)S(1)} all-to-all(bf16[16,640,256]{1,2,0:T(8,128)(2,1)S(1)} %all_to_all.21), channel_id=1, replica_groups=mesh['row'=16,'col'=16] {'col'}, dimensions={0} | all-to-all | bytes 10485760 | tf_op jit(solution)/shard_map/all_to_all | solution.py:27
  211.3 0.0 copy-done
  211.3 7.3 %convolution_bitcast_fusion = f32[640,4096]{0,1:T(8,128)} fusion(bf16[640,4096]{0,1:T(8,128)(2,1)S(1)} %bitcast.15, bf16[640,640]{1,0:T(8,128)(2,1)S(1)} %copy-done), kind=kOutput, calls=%fused_computation | convolution fusion | flops 3355443200 | bytes 16547840 | tf_op jit(solution)/shard_map/dot_general | solution.py:28
  218.7 0.0 copy-start.1
  218.7 0.0 reduce-scatter.3.cloned.1.call-update
  218.7 0.0 reduce-scatter.5.cloned.1.call-start
  218.8 0.1 convert_reduce_fusion
  218.9 207.1 %reduce-scatter.3.cloned.1.call-done = f32[640,256]{0,1:T(8,128)} async-done(((f32[640,4096]{0,1:T(8,128)}), f32[640,256]{0,1:T(8,128)}) %reduce-scatter.3.cloned.1.call-update) | async-done | bytes 655376 | tf_op jit(solution)/shard_map/reduce_scatter | solution.py:29
  426.0 1.1 multiply_convert_fusion
  427.1 1.0 convolution_bitcast_fusion.1
  428.1 0.0 reduce-scatter.5.cloned.1.call-update
  428.2 0.9 copy.9
  429.1 80.6 %reduce-scatter.5.cloned.1.call-done = f32[1,16,256]{2,1,0:T(8,128)} async-done(((f32[1,256,256]{2,1,0:T(8,128)}), f32[1,16,256]{2,1,0:T(8,128)}) %reduce-scatter.5.cloned.1.call-update) | async-done | bytes 16400 | tf_op jit(solution)/shard_map/reduce_scatter | solution.py:36
  509.6 0.0 copy-done.1
  509.6 1.3 sub.3
Async XLA Ops:
  7.2 204.2 %copy-start = (bf16[640,640]{1,0:T(8,128)(2,1)S(1)}, bf16[640,640]{1,0:T(8,128)(2,1)}, u32[]{:S(2)}) copy-start(bf16[640,640]{1,0:T(8,128)(2,1)} %param.4) | copy-start | bytes 2457604
  7.2 418.8 %reduce-scatter.3.cloned.1.call-start = ((), (), s32[]{:S(2)}) async-start(), calls=%async_computation.4 | async-start | bytes 11141120 | tf_op jit(solution)/shard_map/reduce_scatter | solution.py:29
  218.7 290.9 %copy-start.1 = (f32[1,16,256]{2,1,0:T(8,128)S(1)}, f32[1,16,256]{2,1,0:T(8,128)}, u32[]{:S(2)}) copy-start(f32[1,16,256]{2,1,0:T(8,128)} %param.6) | copy-start | bytes 49156
  218.7 290.9 %reduce-scatter.5.cloned.1.call-start = ((), (), s32[]{:S(2)}) async-start(), calls=%async_computation.5 | async-start | bytes 278528 | tf_op jit(solution)/shard_map/reduce_scatter | solution.py:36
Sparse Core Ops, SparseCore 0:
  218.8 207.1 reduce-scatter.2
  428.5 81.1 reduce-scatter.4
